TPU v7x, 256 devices: a whole 4x4x8 slice. The times are simulated.
256 devices in a mesh: row: 8 (over z), col: 16 (over y, x), smp: 2 (over core).
Axes of the slice: x: 4, y: 4, z: 8, core: 2. Of those that a mesh axis runs over, the one named last changes fastest.
Arguments:
- state: float32 [8, 2048, 512], P('smp', ('row', 'col')), may hold values from -6 to 6
- noise: float32 [2, 8, 2048, 512], P(None, 'smp', ('row', 'col')), may hold values from -6 to 6
- pair: bfloat16 [2048, 2048, 128], P('row', 'col'), may hold values from -10 to 10
- contacts: int32 [16, 6], replicated, may hold values from -1 to 15, as said below
- norm_gain: float32 [512], replicated, may hold values from 0.1 to 1.9
- w_qkv: bfloat16 [512, 1536], replicated, may hold values from -0.25 to 0.25
- w_out: bfloat16 [512, 512], replicated, may hold values from -0.25 to 0.25
- w_bias: bfloat16 [128, 32], replicated, may hold values from -1.5 to 1.5
Outputs:
- denoised: float32 [8, 2048, 512], P('smp', ('row', 'col'))
Inputs may be any that keep to these rules, and one draw needn't show every extreme that they name: `contacts`: row q lists distinct blocks, q itself first, then nearby blocks more often than far ones; its first counts are blocks and the remaining slots hold -1; some row uses all 6 slots.
All inputs are finite; a program needn't handle non-finite values.
Results may differ from a plain program's by a relative error of at most 0.012.
Values may be sent and summed in bfloat16 or wider, within the bound.
A program may use at most 128 MiB of HBM per device.

v0:
```python
import jax
import jax.numpy as jnp
from jax import lax
from jax.sharding import PartitionSpec as P

STEPS = 2


def from_root(block, axis, owner):
    block = jnp.where(lax.axis_index(axis) == owner, block, jnp.zeros_like(block))
    return lax.psum(block, axis)


def body(state, noise, pair, contacts, norm_gain, w_qkv, w_out, w_bias):
    samples_dev, rows_dev, width = state.shape
    heads = w_bias.shape[1]
    head_dim = width // heads
    row_span, blk = (pair.shape[0], pair.shape[1])
    per_row = row_span // blk
    half = row_span // lax.axis_size("smp")
    own_rows = lax.dynamic_slice_in_dim(pair, lax.axis_index("smp") * half, half, 0)
    part_bias = jnp.einsum(
        "ijc,ch->hij", own_rows, w_bias, preferred_element_type=jnp.float32
    ).astype(jnp.bfloat16)
    bias = lax.all_gather(part_bias, "smp", axis=1, tiled=True).astype(jnp.float32)
    col_index = lax.axis_index("col")
    row_index = lax.axis_index("row")
    listed = lax.dynamic_slice_in_dim(contacts, row_index * per_row, per_row, 0)
    matched = jnp.any(listed == col_index, axis=1)
    allowed = jnp.repeat(matched, blk, total_repeat_length=row_span)
    busy = jnp.any(matched)
    x = state
    for step in range(STEPS):
        mean = jnp.mean(x, axis=-1, keepdims=True)
        var = jnp.mean((x - mean) ** 2, axis=-1, keepdims=True)
        normed = ((x - mean) * lax.rsqrt(var + 1e-05) * norm_gain).astype(jnp.bfloat16)
        qkv = jnp.dot(normed, w_qkv, preferred_element_type=jnp.float32).astype(jnp.bfloat16)
        block_rows = lax.all_gather(qkv, "col", axis=1, tiled=True)
        offset = col_index % per_row * blk
        mine = lax.dynamic_slice_in_dim(block_rows[..., width:], offset, blk, 1)
        keyval = from_root(mine, "row", col_index // per_row)
        queries = block_rows[..., :width].reshape(samples_dev, row_span, heads, head_dim)
        keys = keyval[..., :width].reshape(samples_dev, blk, heads, head_dim)
        values = keyval[..., width:].reshape(samples_dev, blk, heads, head_dim)

        def attend(unused):
            scores = (
                jnp.einsum("srhd,skhd->hsrk", queries, keys, preferred_element_type=jnp.float32)
                * 0.25
                + bias[:, None]
            )
            m_raw = jnp.max(scores, axis=-1)
            m_blk = jnp.where(allowed[None, None, :], m_raw, jnp.float32(-1e30))
            probs = jnp.where(
                allowed[None, None, :, None], jnp.exp(scores - m_raw[..., None]), jnp.float32(0.0)
            )
            totals = jnp.sum(probs, axis=-1)
            outputs = jnp.einsum(
                "hsrk,skhd->srhd",
                probs.astype(jnp.bfloat16),
                values,
                preferred_element_type=jnp.float32,
            )
            return (
                m_blk.transpose(1, 2, 0),
                totals.transpose(1, 2, 0),
                outputs.reshape(samples_dev, row_span, width),
            )

        def skipped(unused):
            return (
                jnp.full((samples_dev, row_span, heads), -1e30, jnp.float32),
                jnp.zeros((samples_dev, row_span, heads), jnp.float32),
                jnp.zeros((samples_dev, row_span, width), jnp.float32),
            )

        m_blk, totals, outputs = lax.cond(busy, attend, skipped, 0)
        top = lax.pmax(m_blk.astype(jnp.bfloat16), "col").astype(m_blk.dtype)
        weight = jnp.exp(m_blk - top)
        scaled = (
            outputs.reshape(samples_dev, row_span, heads, head_dim) * weight[..., None]
        ).reshape(samples_dev, row_span, width)
        summed, acc = (
            lax.psum_scatter(totals * weight, "col", scatter_dimension=1, tiled=True),
            lax.psum_scatter(scaled, "col", scatter_dimension=1, tiled=True),
        )
        attn = (acc.reshape(samples_dev, rows_dev, heads, head_dim) / summed[..., None]).reshape(
            samples_dev, rows_dev, width
        )
        attn = attn.astype(jnp.bfloat16)
        out = jnp.dot(attn, w_out, preferred_element_type=jnp.float32)
        x = x + out + 0.5 * 0.5**step * noise[step]
    return x


def solution(mesh):
    in_specs = (
        P("smp", ("row", "col"), None),
        P(None, "smp", ("row", "col"), None),
        P("row", "col", None),
        P(),
        P(),
        P(),
        P(),
        P(),
    )
    out_specs = P("smp", ("row", "col"), None)
    return jax.shard_map(body, mesh=mesh, in_specs=in_specs, out_specs=out_specs, check_vma=False)
```

profile of v0, /device:TPU:1, one launch (start us, length us, event | category | flops | bytes accessed | tf_op | source)
XLA Modules:
  0.0 770.3 jit_solution(14538606355737976069)
XLA Ops:
  6.5 1.1 reduce_sum.54
  7.7 1.1 multiply_reduce_fusion.1
  8.7 2.0 convolution_convert_fusion.1
  10.8 4.8 fusion.23
  15.7 51.2 %all-gather.4.cloned.1.call-done = bf16[4,256,1536]{2,1,0:T(8,128)(2,1)} async-done(((bf16[4,16,1536]{2,1,0:T(8,128)(2,1)}), bf16[4,256,1536]{2,1,0:T(8,128)(2,1)}) %all-gather.4.cloned.1.call-update) | async-done | bytes 3145744 | tf_op jit(solution)/shard_map/all_gather | solution.py:38
  66.9 1.6 slice-done
  68.5 1.2 dynamic-slice_select_fusion.1
  71.8 1.2 select_reduce_fusion
  73.0 11.8 %all-gather.6.cloned.1.call-done = bf16[32,256,128]{2,0,1:T(8,128)(2,1)} async-done(((bf16[32,128,128]{2,0,1:T(8,128)(2,1)}), bf16[32,256,128]{2,0,1:T(8,128)(2,1)}) %all-gather.6.cloned.1.call-update) | async-done | bytes 2097168 | tf_op jit(solution)/shard_map/all_gather | solution.py:25
  84.8 4.1 convert_element_type.54
  88.9 70.4 %all-reduce.13.cloned.1.call-done = bf16[4,128,1024]{2,1,0:T(8,128)(2,1)} async-done(((bf16[4,128,1024]{2,1,0:T(8,128)(2,1)}), bf16[4,128,1024]{2,1,0:T(8,128)(2,1)}) %all-reduce.13.cloned.1.call-update) | async-done | bytes 1048592 | tf_op jit(solution)/shard_map/psum | solution.py:11
  159.4 29.7 %conditional.2 = (f32[4,256,512]{1,2,0:T(8,128)}, f32[4,256,32]{1,2,0:T(8,128)}, f32[4,256,32]{1,2,0:T(8,128)}) conditional(s32[]{:T(128)} %convert_element_type.49, () %tuple.25, (pred[256]{0:T(512)(128)(4,1)S(1)}, bf16[4,256,1536]{2,1,0:T(8,128)(2,1)}, bf16[4,128,1024]{2,1,0:T(8,128)(2,1)}, f32[32,256,128]{2,0,1:T(8,128)}) %tuple.26), branch_computations={%region_5.6_spmd, %region_6.9_spmd} | conditional | flops 306151424 | bytes 102367824 | solution.py:77
  159.4 5.3 copy.95
  164.6 1.6 copy.94
  166.3 0.9 fusion.47
  167.1 4.6 copy.93
  171.8 1.3 slice.60
  173.1 5.4 fusion
  178.5 6.6 fusion.2
  186.5 2.6 fusion.3
  189.1 1.5 convert_element_type.55
  190.7 93.2 %all-reduce.15.cloned.1.call-done = bf16[4,256,32]{1,2,0:T(8,128)(2,1)} async-done(((bf16[4,256,32]{1,2,0:T(8,128)(2,1)}), bf16[4,256,32]{1,2,0:T(8,128)(2,1)}) %all-reduce.15.cloned.1.call-update) | async-done | bytes 65552 | tf_op jit(solution)/shard_map/pmax | solution.py:78
  283.9 1.0 fusion.46
  284.9 3.2 bitcast_multiply_fusion.1
  288.1 3.1 copy.98
  291.3 1.1 copy.100
  293.6 102.3 %all-reduce.23.cloned.1.call-done = (f32[4,256,32]{2,0,1:T(4,128)}, f32[4,256,512]{2,0,1:T(4,128)}) async-done(((f32[4,256,32]{2,0,1:T(4,128)}, f32[4,256,512]{2,0,1:T(4,128)}), (f32[4,256,32]{2,0,1:T(4,128)}, f32[4,256,512]{2,0,1:T(4,128)})) %all-reduce.23.cloned.1.call-update) | async-done | bytes 2228240
  396.7 1.6 constant_dynamic-slice_fusion.3
  399.3 1.3 fusion.50
  400.7 1.1 convolution_convert_fusion
  401.9 52.4 %all-gather.8.cloned.1.call-done = bf16[4,256,1536]{2,1,0:T(8,128)(2,1)} async-done(((bf16[4,16,1536]{2,1,0:T(8,128)(2,1)}), bf16[4,256,1536]{2,1,0:T(8,128)(2,1)}) %all-gather.8.cloned.1.call-update) | async-done | bytes 3145744 | tf_op jit(solution)/shard_map/all_gather | solution.py:38
  454.4 1.6 slice-done.1
  456.0 1.2 dynamic-slice_select_fusion
  457.3 71.1 %all-reduce.17.cloned.1.call-done = bf16[4,128,1024]{2,1,0:T(8,128)(2,1)} async-done(((bf16[4,128,1024]{2,1,0:T(8,128)(2,1)}), bf16[4,128,1024]{2,1,0:T(8,128)(2,1)}) %all-reduce.17.cloned.1.call-update) | async-done | bytes 1048592 | tf_op jit(solution)/shard_map/psum | solution.py:11
  528.4 25.1 %conditional.3 = (f32[4,256,512]{1,2,0:T(8,128)}, f32[4,256,32]{1,2,0:T(8,128)S(1)}, f32[4,256,32]{1,2,0:T(8,128)S(1)}) conditional(s32[]{:T(128)} %convert_element_type.49, () %tuple.27, (pred[256]{0:T(512)(128)(4,1)S(1)}, bf16[4,256,1536]{2,1,0:T(8,128)(2,1)}, bf16[4,128,1024]{2,1,0:T(8,128)(2,1)}, f32[32,256,128]{2,0,1:T(8,128)}) %tuple.28), branch_computations={%region_15.16_spmd, %region_16.19_spmd} | conditional | flops 306151424 | bytes 106037840 | solution.py:77
  528.4 5.4 copy.105
  534.5 4.6 copy.103
  539.1 1.3 slice.63
  540.5 4.5 fusion.8
  545.0 5.8 fusion.10
  550.9 2.6 fusion.11
  554.2 93.3 %all-reduce.19.cloned.1.call-done = bf16[4,256,32]{1,2,0:T(8,128)(2,1)} async-done(((bf16[4,256,32]{1,2,0:T(8,128)(2,1)}), bf16[4,256,32]{1,2,0:T(8,128)(2,1)}) %all-reduce.19.cloned.1.call-update) | async-done | bytes 65552 | tf_op jit(solution)/shard_map/pmax | solution.py:78
  648.4 3.1 bitcast_multiply_fusion
  651.5 3.2 copy.108
  654.7 1.0 copy.110
  655.7 103.6 %all-reduce.21.cloned.1.call-done = (f32[4,256,32]{2,0,1:T(4,128)}, f32[4,256,512]{2,0,1:T(4,128)}) async-done(((f32[4,256,32]{2,0,1:T(4,128)}, f32[4,256,512]{2,0,1:T(4,128)}), (f32[4,256,32]{2,0,1:T(4,128)}, f32[4,256,512]{2,0,1:T(4,128)})) %all-reduce.21.cloned.1.call-update) | async-done | bytes 2228240
  760.1 0.9 constant_dynamic-slice_fusion.1
  762.0 1.8 fusion.26
  (71 shorter events, 9.8 us)
Async XLA Ops:
  6.5 2.2 copy-start
  6.5 60.4 %all-gather.4.cloned.1.call-start = ((), (), s32[]{:S(2)}) async-start(), calls=%async_computation | async-start | bytes 3342336 | tf_op jit(solution)/shard_map/all_gather | solution.py:38
  10.8 74.0 %all-gather.6.cloned.1.call-start = ((), (), s32[]{:S(2)}) async-start(), calls=%async_computation.2 | async-start | bytes 3145728 | tf_op jit(solution)/shard_map/all_gather | solution.py:25
  15.6 54.2 %copy-start.9 = (s32[16,6]{0,1:T(8,128)S(1)}, s32[16,6]{0,1:T(8,128)}, u32[]{:S(2)}) copy-start(s32[16,6]{0,1:T(8,128)} %param.17) | copy-start | bytes 1156
  15.6 143.7 %all-reduce.13.cloned.1.call-start = ((), (), s32[]{:S(2)}) async-start(), calls=%async_computation.1 | async-start | bytes 2097152 | tf_op jit(solution)/shard_map/psum | solution.py:11
  66.9 1.6 slice-start
  69.7 214.2 %all-reduce.15.cloned.1.call-start = ((), (), s32[]{:S(2)}) async-start(), calls=%async_computation.3 | async-start | bytes 131072 | tf_op jit(solution)/shard_map/pmax | solution.py:78
  173.1 5.4 copy-start.2
  178.5 6.6 copy-start.6
  190.6 205.4 %all-reduce.23.cloned.1.call-start = ((), (), s32[]{:S(2)}) async-start(), calls=%async_computation.8 | async-start | bytes 5242880
  288.1 4.3 copy-start.10
  288.1 111.2 %copy-start.4 = (f32[4,16,512]{2,1,0:T(8,128)S(1)}, f32[4,16,512]{2,1,0:T(8,128)}, u32[]{:S(2)}) copy-start(f32[4,16,512]{2,1,0:T(8,128)} %param.14) | copy-start | bytes 393220
  288.1 111.2 %copy-start.5 = (bf16[512,512]{1,0:T(8,128)(2,1)S(1)}, bf16[512,512]{1,0:T(8,128)(2,1)}, u32[]{:S(2)}) copy-start(bf16[512,512]{1,0:T(8,128)(2,1)} %param.20) | copy-start | bytes 1572868
  291.2 109.5 %copy-start.8 = (f32[512]{0:T(512)S(1)}, f32[512]{0:T(512)}, u32[]{:S(2)}) copy-start(f32[512]{0:T(512)} %param.18) | copy-start | bytes 6148
  292.3 162.0 %all-gather.8.cloned.1.call-start = ((), (), s32[]{:S(2)}) async-start(), calls=%async_computation.4 | async-start | bytes 3342336 | tf_op jit(solution)/shard_map/all_gather | solution.py:38
  401.9 126.5 %all-reduce.17.cloned.1.call-start = ((), (), s32[]{:S(2)}) async-start(), calls=%async_computation.5 | async-start | bytes 2097152 | tf_op jit(solution)/shard_map/psum | solution.py:11
  454.4 1.6 slice-start.1
  457.2 190.3 %all-reduce.19.cloned.1.call-start = ((), (), s32[]{:S(2)}) async-start(), calls=%async_computation.6 | async-start | bytes 131072 | tf_op jit(solution)/shard_map/pmax | solution.py:78
  528.4 5.4 copy-start.7
  540.4 4.5 copy-start.3
  554.2 205.2 %all-reduce.21.cloned.1.call-start = ((), (), s32[]{:S(2)}) async-start(), calls=%async_computation.7 | async-start | bytes 5242880
  651.5 112.3 %copy-start.1 = (bf16[512,1536]{1,0:T(8,128)(2,1)S(1)}, bf16[512,1536]{1,0:T(8,128)(2,1)}, u32[]{:S(2)}) copy-start(bf16[512,1536]{1,0:T(8,128)(2,1)} %param.19) | copy-start | bytes 4718596
Sparse Core Ops, SparseCore 0:
  10.9 55.9 all-gather.3
  68.7 16.0 all-gather.5
  87.2 72.1 all-reduce.12
  190.7 93.1 all-reduce.14
  292.5 103.4 all-reduce.22
  402.0 52.3 all-gather.7
  457.3 71.0 all-reduce.16
  554.3 93.1 all-reduce.18
  655.8 103.4 all-reduce.20
where the time goes:
time: 771 us; the launch traced here: 770 us
  waiting for transfers between devices  650 us (84%)
  local copies, waits for them, and re-layouts  45.9 us (6%)
  other arithmetic  33.8 us (4%)
  matrix products  26 us (3%)
  between operations  14.7 us (2%)
    unnamed x11, waiting for transfers between devices  206 us
    pmax x2, waiting for transfers between devices, body(): top = lax.pmax(m_blk.astype(jnp.bfloat16), 'col').astype(m_blk.dtype)  187 us
    psum x2, waiting for transfers between devices, from_root(): return lax.psum(block, axis)  142 us
    all_gather x2, waiting for transfers between devices, body(): block_rows = lax.all_gather(qkv, 'col', axis=1, tiled=True)  104 us
    another operation x6, local copies, waits for them, and re-layouts  22.2 us
  transfers between devices with their start and end apart: 9, of which 9 were waited for; matrix products, arithmetic and copies ran while one was open for 2% of the time, Pallas kernels for 0%

commit v1 on v0

--- a/solution.py
+++ b/solution.py
@@ -2,6 +2,7 @@
 import jax.numpy as jnp
 from jax import lax
 from jax.sharding import PartitionSpec as P
+from jax.lax import all_to_all, axis_size
 
 STEPS = 2
 
@@ -35,7 +36,10 @@
         var = jnp.mean((x - mean) ** 2, axis=-1, keepdims=True)
         normed = ((x - mean) * lax.rsqrt(var + 1e-05) * norm_gain).astype(jnp.bfloat16)
         qkv = jnp.dot(normed, w_qkv, preferred_element_type=jnp.float32).astype(jnp.bfloat16)
-        block_rows = lax.all_gather(qkv, "col", axis=1, tiled=True)
+        indices_carry = lambda slab_in, dev_axis, join_dim: jnp.concatenate(
+            all_to_all(jnp.stack([slab_in] * axis_size(dev_axis)), dev_axis, 0, 0), axis=join_dim
+        )
+        block_rows = indices_carry(qkv, "col", 1)
         offset = col_index % per_row * blk
         mine = lax.dynamic_slice_in_dim(block_rows[..., width:], offset, blk, 1)
         keyval = from_root(mine, "row", col_index // per_row)

time: 771 us -> 747 us (0.969)
  waiting for transfers between devices: 650 us -> 569 us
  blocking collectives: 0 us -> 42.6 us
    all_gather x2 -> x0, waiting for transfers between devices: 104 us -> none  [body(): block_rows = lax.all_gather(qkv, 'col', axis=1, tiled=True)]
    all_to_all x0 -> x1, blocking collectives: none -> 42.6 us  [body(): all_to_all(jnp.stack([slab_in] * axis_size(dev_axis)), dev_axis, 0, 0)]
    all_to_all x0 -> x1, waiting for transfers between devices: none -> 42 us  [body(): all_to_all(jnp.stack([slab_in] * axis_size(dev_axis)), dev_axis, 0, 0)]
    all_gather x1, waiting for transfers between devices: 11.8 us -> 0.02 us  [body(): lax.all_gather(part_bias, 'smp', axis=1, tiled=True).astype(jnp.float32)]
    another operation x6 -> x8, local copies, waits for them, and re-layouts: 22.2 us -> 24.6 us
    unnamed x11 -> x9, waiting for transfers between devices: 206 us -> 205 us
  transfers between devices with their start and end apart: 9 -> 8, of which waited for: 9 -> 7; matrix products, arithmetic and copies ran while one was open for 2% -> 2% of each run, Pallas kernels for 0% -> 0%
where the time goes in v1:
time: 747 us; the launch traced here: 746 us
  waiting for transfers between devices  569 us (76%)
  local copies, waits for them, and re-layouts  51.5 us (7%)
  blocking collectives  42.6 us (6%)
  other arithmetic  33.8 us (5%)
  matrix products  24.5 us (3%)
  between operations  16.5 us (2%)
  starting transfers between devices  7.92 us (1%)
    unnamed x9, waiting for transfers between devices  205 us
    pmax x2, waiting for transfers between devices, body(): top = lax.pmax(m_blk.astype(jnp.bfloat16), 'col').astype(m_blk.dtype)  186 us
    psum x2, waiting for transfers between devices, from_root(): return lax.psum(block, axis)  136 us
    all_to_all x1, blocking collectives, body(): all_to_all(jnp.stack([slab_in] * axis_size(dev_axis)), dev_axis, 0, 0)  42.6 us
    all_to_all x1, waiting for transfers between devices, body(): all_to_all(jnp.stack([slab_in] * axis_size(dev_axis)), dev_axis, 0, 0)  42 us
    another operation x6, local copies, waits for them, and re-layouts  22.2 us
  transfers between devices with their start and end apart: 8, of which 7 were waited for; matrix products, arithmetic and copies ran while one was open for 2% of the time, Pallas kernels for 0%

profile of v1, /device:TPU:1, one launch (start us, length us, event | category | flops | bytes accessed | tf_op | source)
XLA Modules:
  0.0 746.0 jit_solution(9172947712839519341)
XLA Ops:
  7.4 1.1 reduce_sum.54
  8.5 1.1 multiply_reduce_fusion.1
  9.6 1.3 convolution_convert_fusion.1
  10.9 2.1 stack.4
  13.0 7.6 %all-to-all-start = ((bf16[16,4,16,1536]{3,2,1,0:T(8,128)(2,1)}), bf16[16,4,16,1536]{3,2,1,0:T(8,128)(2,1)}, u32[]{:S(2)}, u32[]{:S(2)}) async-start(bf16[16,4,16,1536]{3,2,1,0:T(8,128)(2,1)} %stack.4), calls=%async_computation | async-start | bytes 6291456 | tf_op jit(solution)/shard_map/all_to_all | solution.py:40
  20.7 4.7 fusion.23
  25.5 42.0 %all-to-all-done = bf16[16,4,16,1536]{3,2,1,0:T(8,128)(2,1)} async-done(((bf16[16,4,16,1536]{3,2,1,0:T(8,128)(2,1)}), bf16[16,4,16,1536]{3,2,1,0:T(8,128)(2,1)}, u32[]{:S(2)}, u32[]{:S(2)}) %all-to-all-start) | async-done | bytes 3145760 | tf_op jit(solution)/shard_map/all_to_all | solution.py:40
  67.5 2.1 copy.98
  69.7 1.7 copy-done.4
  71.7 1.2 dynamic-slice_select_fusion.1
  75.0 1.3 select_reduce_fusion
  76.3 4.1 convert_element_type.54
  80.4 65.2 %all-reduce.13.cloned.1.call-done = bf16[4,128,1024]{2,1,0:T(8,128)(2,1)} async-done(((bf16[4,128,1024]{2,1,0:T(8,128)(2,1)}), bf16[4,128,1024]{2,1,0:T(8,128)(2,1)}) %all-reduce.13.cloned.1.call-update) | async-done | bytes 1048592 | tf_op jit(solution)/shard_map/psum | solution.py:12
  145.6 29.6 %conditional.2 = (f32[4,256,512]{1,2,0:T(8,128)}, f32[4,256,32]{1,2,0:T(8,128)}, f32[4,256,32]{1,2,0:T(8,128)}) conditional(s32[]{:T(128)} %convert_element_type.49, () %tuple.25, (pred[256]{0:T(512)(128)(4,1)S(1)}, bf16[4,256,1536]{2,1,0:T(8,128)(2,1)}, bf16[4,128,1024]{2,1,0:T(8,128)(2,1)}, f32[32,256,128]{2,0,1:T(8,128)}) %tuple.78), branch_computations={%region_5.6_spmd, %region_6.9_spmd} | conditional | flops 306151424 | bytes 102367824 | solution.py:81
  145.6 5.3 copy.101
  150.9 1.6 copy.100
  153.4 4.6 copy.99
  158.0 1.3 slice.60
  159.3 5.3 fusion
  164.6 6.6 fusion.2
  172.6 2.5 fusion.3
  175.2 1.5 convert_element_type.55
  176.8 93.1 %all-reduce.15.cloned.1.call-done = bf16[4,256,32]{1,2,0:T(8,128)(2,1)} async-done(((bf16[4,256,32]{1,2,0:T(8,128)(2,1)}), bf16[4,256,32]{1,2,0:T(8,128)(2,1)}) %all-reduce.15.cloned.1.call-update) | async-done | bytes 65552 | tf_op jit(solution)/shard_map/pmax | solution.py:82
  269.9 1.0 fusion.46
  270.9 3.2 bitcast_multiply_fusion.1
  274.1 3.1 copy.104
  277.2 1.0 copy.106
  279.6 101.9 %all-reduce.23.cloned.1.call-done = (f32[4,256,32]{2,0,1:T(4,128)}, f32[4,256,512]{2,0,1:T(4,128)}) async-done(((f32[4,256,32]{2,0,1:T(4,128)}, f32[4,256,512]{2,0,1:T(4,128)}), (f32[4,256,32]{2,0,1:T(4,128)}, f32[4,256,512]{2,0,1:T(4,128)})) %all-reduce.23.cloned.1.call-update) | async-done | bytes 2228240
  382.3 1.6 constant_dynamic-slice_fusion.3
  384.8 1.3 fusion.50
  387.1 42.6 %all_to_all.10 = bf16[16,4,16,1536]{3,2,1,0:T(8,128)(2,1)S(1)} all-to-all(bf16[16,4,16,1536]{3,2,1,0:T(8,128)(2,1)S(1)} %stack.5), channel_id=1, replica_groups=mesh['row'=8,'col'=16,'smp'=2] {'col'}, dimensions={0} | all-to-all | bytes 6291456 | tf_op jit(solution)/shard_map/all_to_all | solution.py:40
  430.0 1.7 copy-done.5
  432.0 1.2 dynamic-slice_select_fusion
  433.3 70.5 %all-reduce.17.cloned.1.call-done = bf16[4,128,1024]{2,1,0:T(8,128)(2,1)} async-done(((bf16[4,128,1024]{2,1,0:T(8,128)(2,1)}), bf16[4,128,1024]{2,1,0:T(8,128)(2,1)}) %all-reduce.17.cloned.1.call-update) | async-done | bytes 1048592 | tf_op jit(solution)/shard_map/psum | solution.py:12
  503.8 25.1 %conditional.3 = (f32[4,256,512]{1,2,0:T(8,128)}, f32[4,256,32]{1,2,0:T(8,128)S(1)}, f32[4,256,32]{1,2,0:T(8,128)S(1)}) conditional(s32[]{:T(128)} %convert_element_type.49, () %tuple.27, (pred[256]{0:T(512)(128)(4,1)S(1)}, bf16[4,256,1536]{2,1,0:T(8,128)(2,1)}, bf16[4,128,1024]{2,1,0:T(8,128)(2,1)}, f32[32,256,128]{2,0,1:T(8,128)}) %tuple.79), branch_computations={%region_15.16_spmd, %region_16.19_spmd} | conditional | flops 306151424 | bytes 106037840 | solution.py:81
  503.8 5.4 copy.112
  509.9 4.6 copy.110
  514.5 1.3 slice.63
  515.8 4.5 fusion.8
  520.4 5.8 fusion.10
  526.3 2.6 fusion.11
  529.6 93.1 %all-reduce.19.cloned.1.call-done = bf16[4,256,32]{1,2,0:T(8,128)(2,1)} async-done(((bf16[4,256,32]{1,2,0:T(8,128)(2,1)}), bf16[4,256,32]{1,2,0:T(8,128)(2,1)}) %all-reduce.19.cloned.1.call-update) | async-done | bytes 65552 | tf_op jit(solution)/shard_map/pmax | solution.py:82
  623.5 3.1 bitcast_multiply_fusion
  626.6 3.2 copy.115
  629.8 1.0 copy.117
  630.9 103.2 %all-reduce.21.cloned.1.call-done = (f32[4,256,32]{2,0,1:T(4,128)}, f32[4,256,512]{2,0,1:T(4,128)}) async-done(((f32[4,256,32]{2,0,1:T(4,128)}, f32[4,256,512]{2,0,1:T(4,128)}), (f32[4,256,32]{2,0,1:T(4,128)}, f32[4,256,512]{2,0,1:T(4,128)})) %all-reduce.21.cloned.1.call-update) | async-done | bytes 2228240
  734.9 0.9 constant_dynamic-slice_fusion.1
  736.8 1.8 fusion.26
  (76 shorter events, 12.3 us)
Async XLA Ops:
  7.4 2.2 copy-start
  10.9 9.8 %copy-start.10 = (bf16[128,32]{0,1:T(8,128)(2,1)S(1)}, bf16[128,32]{0,1:T(8,128)(2,1)}, u32[]{:S(2)}) copy-start(bf16[128,32]{0,1:T(8,128)(2,1)} %param.21) | copy-start | bytes 24580
  13.0 54.5 %all-to-all-start = ((bf16[16,4,16,1536]{3,2,1,0:T(8,128)(2,1)}), bf16[16,4,16,1536]{3,2,1,0:T(8,128)(2,1)}, u32[]{:S(2)}, u32[]{:S(2)}) async-start(bf16[16,4,16,1536]{3,2,1,0:T(8,128)(2,1)} %stack.4), calls=%async_computation | async-start | bytes 6291456 | tf_op jit(solution)/shard_map/all_to_all | solution.py:40
  20.6 55.7 %all-gather.2.cloned.1.call-start = ((), (), s32[]{:S(2)}) async-start(), calls=%async_computation.3 | async-start | bytes 3145728 | tf_op jit(solution)/shard_map/all_gather | solution.py:26
  25.4 120.2 %all-reduce.13.cloned.1.call-start = ((), (), s32[]{:S(2)}) async-start(), calls=%async_computation.2 | async-start | bytes 2097152 | tf_op jit(solution)/shard_map/psum | solution.py:12
  69.7 1.7 copy-start.4
  69.7 3.3 copy-start.12
  72.9 196.9 %all-reduce.15.cloned.1.call-start = ((), (), s32[]{:S(2)}) async-start(), calls=%async_computation.4 | async-start | bytes 131072 | tf_op jit(solution)/shard_map/pmax | solution.py:82
  159.3 5.4 copy-start.2
  164.6 6.6 copy-start.8
  176.7 204.8 %all-reduce.23.cloned.1.call-start = ((), (), s32[]{:S(2)}) async-start(), calls=%async_computation.8 | async-start | bytes 5242880
  274.1 4.3 copy-start.13
  274.1 110.7 %copy-start.6 = (f32[4,16,512]{2,1,0:T(8,128)S(1)}, f32[4,16,512]{2,1,0:T(8,128)}, u32[]{:S(2)}) copy-start(f32[4,16,512]{2,1,0:T(8,128)} %param.14) | copy-start | bytes 393220
  274.1 110.7 %copy-start.7 = (bf16[512,512]{1,0:T(8,128)(2,1)S(1)}, bf16[512,512]{1,0:T(8,128)(2,1)}, u32[]{:S(2)}) copy-start(bf16[512,512]{1,0:T(8,128)(2,1)} %param.20) | copy-start | bytes 1572868
  277.2 109.0 %copy-start.11 = (f32[512]{0:T(512)S(1)}, f32[512]{0:T(512)}, u32[]{:S(2)}) copy-start(f32[512]{0:T(512)} %param.18) | copy-start | bytes 6148
  278.3 225.5 %all-reduce.17.cloned.1.call-start = ((), (), s32[]{:S(2)}) async-start(), calls=%async_computation.5 | async-start | bytes 2097152 | tf_op jit(solution)/shard_map/psum | solution.py:12
  430.0 1.7 copy-start.5
  433.2 189.4 %all-reduce.19.cloned.1.call-start = ((), (), s32[]{:S(2)}) async-start(), calls=%async_computation.6 | async-start | bytes 131072 | tf_op jit(solution)/shard_map/pmax | solution.py:82
  503.8 5.4 copy-start.9
  515.8 4.6 copy-start.3
  529.5 204.6 %all-reduce.21.cloned.1.call-start = ((), (), s32[]{:S(2)}) async-start(), calls=%async_computation.7 | async-start | bytes 5242880
  626.6 111.9 %copy-start.1 = (bf16[512,1536]{1,0:T(8,128)(2,1)S(1)}, bf16[512,1536]{1,0:T(8,128)(2,1)}, u32[]{:S(2)}) copy-start(bf16[512,1536]{1,0:T(8,128)(2,1)} %param.19) | copy-start | bytes 4718596
Sparse Core Ops, SparseCore 0:
  25.5 20.0 all-gather.1
Sparse Core Ops, SparseCore 1:
  73.0 72.5 all-reduce.12
  176.8 93.0 all-reduce.14
  278.4 103.1 all-reduce.22
  433.3 70.4 all-reduce.16
  529.6 93.0 all-reduce.18
  631.0 103.1 all-reduce.20
